TPU v7x, 32 devices: a whole 2x2x4 slice. The times are simulated.
32 devices in a mesh: rep: 4 (over z), fsdp: 2 (over x), ctx: 4 (over y, core).
Axes of the slice: x: 2, y: 2, z: 4, core: 2. Of those that a mesh axis runs over, the one named last changes fastest.
Arguments:
- q_proj: bfloat16 [16, 256, 4096], P(('rep', 'fsdp'), 'ctx'), may hold values from -24 to 24
- k_proj: bfloat16 [16, 256, 512], P(('rep', 'fsdp'), 'ctx'), may hold values from -24 to 24
- v_proj: bfloat16 [16, 256, 512], P(('rep', 'fsdp'), 'ctx'), may hold values from -6 to 6
- attn_out: bfloat16 [16, 256, 4096], P(('rep', 'fsdp'), 'ctx'), may hold values from -6 to 6
- upstream: bfloat16 [16, 256, 4096], P(('rep', 'fsdp'), 'ctx'), may hold values from -6 to 6
- advantage: float32 [16, 256], P(('rep', 'fsdp'), 'ctx'), may hold values from -4 to 4
- action_mask: int32 [16, 256], P(('rep', 'fsdp'), 'ctx'), may hold values 0 or 1
- segment_ids: int32 [16, 256], P(('rep', 'fsdp'), 'ctx'), may hold values from 0 to 3, never falling along the last dimension, each value on 1 to 128 neighbouring positions
- codebook: int32 [16, 256], P(('rep', 'fsdp'), 'ctx'), may hold values from 0 to 8, as said below
Outputs:
- grad_q: bfloat16 [16, 256, 4096], P(('rep', 'fsdp'), 'ctx')
- grad_k: bfloat16 [16, 256, 512], P(('rep', 'fsdp'), 'ctx')
- grad_v: bfloat16 [16, 256, 512], P(('rep', 'fsdp'), 'ctx')
- grad_bias_q: float32 [4096], P('fsdp')
- grad_bias_k: float32 [512], P('fsdp')
- grad_bias_v: float32 [512], P('fsdp')
Inputs may be any that keep to these rules, and one draw needn't show every extreme that they name: `codebook`: tokens come in aligned blocks of 8 positions of a dialogue; each block is text (all 0) or one speech frame holding codebooks 1 to 8 in order.
All inputs are finite; a program needn't handle non-finite values. No bound on the sum of `action_mask` on one device may be relied on, other than what follows from the above.
Results may differ from a plain program's by a relative error of at most 0.012.
The roundings to bfloat16 on the way count: a program that leaves them out, or rounds other values in their place, can miss the bound.
Values may be sent and summed in bfloat16 or wider, within the bound.
A program may use at most 64 MiB of HBM per device.

v0:
```python
import math

import jax
import jax.numpy as jnp
from jax import lax
from jax.sharding import PartitionSpec as P

HQ = 32
HK = 4
HD = 128


ROPE_BASE = 1000000.0


def entering(value, axis, join, neutral):
    count, mine = (lax.axis_size(axis), lax.axis_index(axis))
    pieces = lax.all_gather(value, axis)
    subtotal = jnp.full_like(value, 0) + jnp.asarray(neutral, value.dtype)

    def step(position, subtotal):
        longer = join(subtotal, pieces[position])
        return jnp.where(position < mine, longer, subtotal)

    return lax.fori_loop(0, count - 1, step, subtotal)


def rotary_tables(positions):
    half_width = HD // 2
    steps = jnp.arange(half_width, dtype=jnp.float32)
    inverse = jnp.exp(steps * (-2.0 * math.log(ROPE_BASE) / HD))
    angles = positions.astype(jnp.float32)[..., None] * inverse
    return (jnp.cos(angles), jnp.sin(angles))


def rotate(inputs, cosine_table, sine_table):
    half_width = inputs.shape[-1] // 2
    first_half = inputs[..., :half_width]
    second = inputs[..., half_width:]
    cos_rows = cosine_table[..., None, :]
    sin_rows = sine_table[..., None, :]
    return jnp.concatenate(
        [first_half * cos_rows - second * sin_rows, second * cos_rows + first_half * sin_rows],
        axis=-1,
    )


def add_counts(earlier, later):
    return earlier + later


def per_device(
    q_proj, k_proj, v_proj, attn_out, upstream, advantage, action_mask, segment_ids, codebook
):
    seqs = q_proj.shape[0]
    token_list = q_proj.shape[1]
    ctx_size = lax.axis_size("ctx")
    local_heads = HQ // ctx_size
    copies = ctx_size // HK
    length = token_list * ctx_size
    softmax_scale = HD ** (-0.5)
    starts = (codebook <= 1).astype(jnp.int32)
    offset = entering(jnp.sum(starts, axis=1), "ctx", add_counts, jnp.zeros((seqs,), jnp.int32))
    positions = (offset[:, None] + jnp.cumsum(starts, axis=1) - 1).astype(jnp.int32)
    cosine_table, sine_table = rotary_tables(positions)
    q_rot = rotate(
        q_proj.reshape(seqs, token_list, HQ, HD).astype(jnp.float32), cosine_table, sine_table
    ).astype(jnp.bfloat16)
    k_rot = rotate(
        k_proj.reshape(seqs, token_list, HK, HD).astype(jnp.float32), cosine_table, sine_table
    ).astype(jnp.bfloat16)
    k_wide = jnp.broadcast_to(k_rot[:, :, :, None, :], (seqs, token_list, HK, copies, HD)).reshape(
        seqs, token_list, ctx_size, HD
    )
    v_rows = v_proj.reshape(seqs, token_list, HK, HD)
    v_wide = jnp.broadcast_to(v_rows[:, :, :, None, :], (seqs, token_list, HK, copies, HD)).reshape(
        seqs, token_list, ctx_size, HD
    )
    weight = advantage * action_mask.astype(jnp.float32)
    grad_out = (
        (weight[:, :, None] * upstream.astype(jnp.float32))
        .astype(jnp.bfloat16)
        .reshape(seqs, token_list, HQ, HD)
    )
    outputs = attn_out.reshape(seqs, token_list, HQ, HD)
    delta_rows = jnp.sum(grad_out.astype(jnp.float32) * outputs.astype(jnp.float32), axis=-1)
    q_heads, k_heads, v_heads, g_heads = (
        lax.all_to_all(q_rot, "ctx", split_axis=2, concat_axis=1, tiled=True),
        lax.all_to_all(k_wide, "ctx", split_axis=2, concat_axis=1, tiled=True),
        lax.all_to_all(v_wide, "ctx", split_axis=2, concat_axis=1, tiled=True),
        lax.all_to_all(grad_out, "ctx", split_axis=2, concat_axis=1, tiled=True),
    )
    delta_heads = lax.all_to_all(delta_rows, "ctx", split_axis=2, concat_axis=1, tiled=True)
    key_rows = k_heads[:, :, 0, :]
    value_rows = v_heads[:, :, 0, :]
    seg_all = lax.all_gather(segment_ids, "ctx", axis=1, tiled=True)
    row_index = jnp.arange(length)
    block_rows = length // 8

    def one_head(head_slot, state_tuple):
        grad_q_all, grad_k_sum, grad_v_sum = state_tuple
        q_one = lax.dynamic_index_in_dim(q_heads, head_slot, 2, False)
        g_one = lax.dynamic_index_in_dim(g_heads, head_slot, 2, False)
        d_one = lax.dynamic_index_in_dim(delta_heads, head_slot, 2, False)
        pieces = []
        for number in range(8):
            row_low = number * block_rows
            row_high = row_low + block_rows
            query_block_rows = q_one[:, row_low:row_high]
            gradient_block_rows = g_one[:, row_low:row_high]
            d_block = d_one[:, row_low:row_high]
            key_block_rows = key_rows[:, :row_high]
            value_block_rows = value_rows[:, :row_high]
            causal = row_index[None, :row_high] <= row_index[row_low:row_high, None]
            allowed = (seg_all[:, row_low:row_high, None] == seg_all[:, None, :row_high]) & causal[
                None
            ]
            scores = (
                jnp.einsum(
                    "vlf,vwf->vlw",
                    query_block_rows,
                    key_block_rows,
                    preferred_element_type=jnp.float32,
                )
                * softmax_scale
            )
            scores = jnp.where(allowed, scores, -jnp.inf)
            row_max = jnp.max(scores, axis=2, keepdims=True)
            row_total = jnp.sum(jnp.exp(scores - row_max), axis=2, keepdims=True)
            attention = jnp.exp(scores - (row_max + jnp.log(row_total)))
            attention_reduced_precision = attention.astype(jnp.bfloat16)
            grad_v_sum = grad_v_sum.at[:, :row_high].add(
                jnp.einsum(
                    "lox,log->lxg",
                    attention_reduced_precision,
                    gradient_block_rows,
                    preferred_element_type=jnp.float32,
                )
            )
            grad_probs = jnp.einsum(
                "vlf,vwf->vlw",
                gradient_block_rows,
                value_block_rows,
                preferred_element_type=jnp.float32,
            )
            scores_gradient = (attention * (grad_probs - d_block[:, :, None])).astype(jnp.bfloat16)
            pieces.append(
                jnp.einsum(
                    "uwa,uai->uwi",
                    scores_gradient,
                    key_block_rows,
                    preferred_element_type=jnp.float32,
                )
                * softmax_scale
            )
            grad_k_sum = grad_k_sum.at[:, :row_high].add(
                jnp.einsum(
                    "lox,log->lxg",
                    scores_gradient,
                    query_block_rows,
                    preferred_element_type=jnp.float32,
                )
                * softmax_scale
            )
        grad_q_all = lax.dynamic_update_index_in_dim(
            grad_q_all, jnp.concatenate(pieces, axis=1), head_slot, 2
        )
        return (grad_q_all, grad_k_sum, grad_v_sum)

    start_state = (
        jnp.zeros((seqs, length, local_heads, HD), jnp.float32),
        jnp.zeros((seqs, length, HD), jnp.float32),
        jnp.zeros((seqs, length, HD), jnp.float32),
    )
    grad_q_all, grad_k_sum, grad_v_sum = lax.fori_loop(0, local_heads, one_head, start_state)
    grad_q_tok, grad_k_wide, grad_v_wide = (
        lax.all_to_all(grad_q_all, "ctx", split_axis=1, concat_axis=2, tiled=True),
        lax.all_to_all(grad_k_sum[:, :, None, :], "ctx", split_axis=1, concat_axis=2, tiled=True),
        lax.all_to_all(grad_v_sum[:, :, None, :], "ctx", split_axis=1, concat_axis=2, tiled=True),
    )
    grad_q = (
        rotate(grad_q_tok, cosine_table, -sine_table)
        .astype(jnp.bfloat16)
        .reshape(seqs, token_list, HQ * HD)
    )
    grad_k_tok = jnp.sum(grad_k_wide.reshape(seqs, token_list, HK, copies, HD), axis=3)
    grad_v_tok = jnp.sum(grad_v_wide.reshape(seqs, token_list, HK, copies, HD), axis=3)
    grad_k = (
        rotate(grad_k_tok, cosine_table, -sine_table)
        .astype(jnp.bfloat16)
        .reshape(seqs, token_list, HK * HD)
    )
    grad_v = grad_v_tok.astype(jnp.bfloat16).reshape(seqs, token_list, HK * HD)
    part_q = jnp.sum(grad_q.astype(jnp.float32), axis=(0, 1))
    part_k = jnp.sum(grad_k.astype(jnp.float32), axis=(0, 1))
    part_v = jnp.sum(grad_v.astype(jnp.float32), axis=(0, 1))
    summed = lax.psum((part_q, part_k, part_v), "ctx")
    shares = (
        lax.psum_scatter(summed[0], "fsdp", scatter_dimension=0, tiled=True),
        lax.psum_scatter(summed[1], "fsdp", scatter_dimension=0, tiled=True),
        lax.psum_scatter(summed[2], "fsdp", scatter_dimension=0, tiled=True),
    )
    bias_q, bias_k, bias_v = lax.psum((shares[0], shares[1], shares[2]), "rep")
    return (grad_q, grad_k, grad_v, bias_q, bias_k, bias_v)


def solution(mesh):
    placed = (
        P(("rep", "fsdp"), "ctx", None),
        P(("rep", "fsdp"), "ctx", None),
        P(("rep", "fsdp"), "ctx", None),
        P(("rep", "fsdp"), "ctx", None),
        P(("rep", "fsdp"), "ctx", None),
        P(("rep", "fsdp"), "ctx"),
        P(("rep", "fsdp"), "ctx"),
        P(("rep", "fsdp"), "ctx"),
        P(("rep", "fsdp"), "ctx"),
    )
    return jax.shard_map(
        per_device,
        mesh=mesh,
        in_specs=placed,
        out_specs=(
            P(("rep", "fsdp"), "ctx", None),
            P(("rep", "fsdp"), "ctx", None),
            P(("rep", "fsdp"), "ctx", None),
            P("fsdp"),
            P("fsdp"),
            P("fsdp"),
        ),
        check_vma=False,
    )
```

profile of v0, /device:TPU:4, one launch (start us, length us, event | category | flops | bytes accessed | tf_op | source)
XLA Modules:
  0.0 268.4 jit_solution(15221920988417092293)
XLA Ops:
  1.4 1.6 multiply_convert_fusion
  5.0 3.3 %all-to-all-start.4 = ((f32[4,1,1024]{2,1,0:T(1,128)}), f32[4,1,1024]{2,1,0:T(1,128)S(1)}, u32[]{:S(2)}, u32[]{:S(2)}) async-start(f32[4,1,1024]{2,1,0:T(1,128)} %reshape.1247), calls=%async_computation.4 | async-start | bytes 32768 | tf_op jit(solution)/shard_map/all_to_all | solution.py:93
  10.4 4.3 %all-reduce = s32[8]{0:T(128)S(1)} all-reduce(s32[8]{0:T(128)S(1)} %dynamic-update-slice.144), channel_id=2, replica_groups=mesh['rep'=4,'fsdp'=2,'ctx'=4] {'ctx'}, use_global_device_ids=true, to_apply=%add | all-reduce | flops 8 | bytes 64
  17.7 1.6 fusion.133
  19.3 1.8 subtract_convert_fusion
  22.3 4.5 %all-to-all-start.1 = ((bf16[2,64,4,128]{3,1,0,2:T(8,128)(2,1)}), bf16[2,64,4,128]{3,1,0,2:T(8,128)(2,1)S(1)}, u32[]{:S(2)}, u32[]{:S(2)}) async-start(bf16[2,64,4,128]{3,1,0,2:T(8,128)(2,1)} %copy.91), calls=%async_computation.1 | async-start | bytes 262144 | tf_op jit(solution)/shard_map/all_to_all | solution.py:89
  27.4 2.3 all-to-all-done.1
  29.7 5.5 %all-to-all-start.3 = ((bf16[2,64,4,128]{3,1,0,2:T(8,128)(2,1)}), bf16[2,64,4,128]{3,1,0,2:T(8,128)(2,1)}, u32[]{:S(2)}, u32[]{:S(2)}) async-start(bf16[2,64,4,128]{3,1,0,2:T(8,128)(2,1)} %copy_bitcast_fusion.5), calls=%async_computation.3 | async-start | bytes 262144 | tf_op jit(solution)/shard_map/all_to_all | solution.py:90
  35.8 1.4 copy.89
  38.3 5.1 %all-to-all-start = ((bf16[2,64,32,128]{3,1,0,2:T(8,128)(2,1)}), bf16[2,64,32,128]{3,1,0,2:T(8,128)(2,1)S(1)}, u32[]{:S(2)}, u32[]{:S(2)}) async-start(bf16[2,64,32,128]{3,1,0,2:T(8,128)(2,1)} %copy.89), calls=%async_computation | async-start | bytes 2097152 | tf_op jit(solution)/shard_map/all_to_all | solution.py:88
  43.4 1.3 copy_bitcast_fusion.1
  44.8 11.5 %all-to-all-done = bf16[2,64,32,128]{3,1,0,2:T(8,128)(2,1)S(1)} async-done(((bf16[2,64,32,128]{3,1,0,2:T(8,128)(2,1)}), bf16[2,64,32,128]{3,1,0,2:T(8,128)(2,1)S(1)}, u32[]{:S(2)}, u32[]{:S(2)}) %all-to-all-start) | async-done | bytes 1048608 | tf_op jit(solution)/shard_map/all_to_all | solution.py:88
  56.2 5.1 %all-to-all-start.2 = ((bf16[2,64,32,128]{3,1,0,2:T(8,128)(2,1)}), bf16[2,64,32,128]{3,1,0,2:T(8,128)(2,1)S(1)}, u32[]{:S(2)}, u32[]{:S(2)}) async-start(bf16[2,64,32,128]{3,1,0,2:T(8,128)(2,1)} %copy_bitcast_fusion.1), calls=%async_computation.2 | async-start | bytes 2097152 | tf_op jit(solution)/shard_map/all_to_all | solution.py:91
  61.4 13.7 %all-gather.1 = s32[4,64,2]{1,2,0:T(2,128)S(1)} all-gather(s32[1,64,2]{1,2,0:T(2,128)S(1)} %bitcast.219), channel_id=1, replica_groups=mesh['rep'=4,'fsdp'=2,'ctx'=4] {'ctx'}, dimensions={0}, use_global_device_ids=true | all-gather | bytes 2560 | tf_op jit(solution)/shard_map/all_gather | solution.py:96
  79.5 100.9 %while.68 = (s32[]{:T(128)}, f32[2,256,8,128]{3,0,2,1:T(2,128)}, f32[2,256,128]{2,1,0:T(8,128)S(1)}, f32[2,256,128]{2,1,0:T(8,128)S(1)}, s32[2,256]{1,0:T(2,128)...) while((s32[]{:T(128)}, f32[2,256,8,128]{3,0,2,1:T(2,128)}, ...), condition=%wide.region_22.23_spmd.clone.clone, body=%wide.region_5.22_spmd.clone.clone.sunk | while | flops 96448000 | bytes 11459343 | solution.py:175
  181.3 4.9 %all-to-all-start.7 = ((bf16[2,256,1,128]{3,0,2,1:T(2,128)(2,1)}), bf16[2,256,1,128]{3,0,2,1:T(2,128)(2,1)S(1)}, u32[]{:S(2)}, u32[]{:S(2)}) async-start(bf16[2,256,1,128]{3,0,2,1:T(2,128)(2,1)} %bitcast.118), calls=%async_computation.7 | async-start | bytes 262144 | tf_op jit(solution)/shard_map/all_to_all | solution.py:179
  186.4 2.8 %all-to-all-done.7 = bf16[2,256,1,128]{3,0,2,1:T(2,128)(2,1)S(1)} async-done(((bf16[2,256,1,128]{3,0,2,1:T(2,128)(2,1)}), bf16[2,256,1,128]{3,0,2,1:T(2,128)(2,1)S(1)}, u32[]{:S(2)}, u32[]{:S(2)}) %all-to-all-start.7) | async-done | bytes 131104 | tf_op jit(solution)/shard_map/all_to_all | solution.py:179
  189.2 8.4 %all_to_all.126 = f32[2,256,1,128]{3,0,2,1:T(2,128)S(1)} all-to-all(f32[2,256,1,128]{3,0,2,1:T(2,128)S(1)} %bitcast.212), channel_id=1, replica_groups=mesh['rep'=4,'fsdp'=2,'ctx'=4] {'ctx'}, dimensions={1} | all-to-all | bytes 524288 | tf_op jit(solution)/shard_map/all_to_all | solution.py:178
  197.5 5.3 %all-to-all-start.5 = ((f32[2,256,8,128]{3,0,2,1:T(2,128)}), f32[2,256,8,128]{3,0,2,1:T(2,128)S(1)}, u32[]{:S(2)}, u32[]{:S(2)}) async-start(f32[2,256,8,128]{3,0,2,1:T(2,128)} %get-tuple-element.751), calls=%async_computation.5 | async-start | bytes 4194304 | tf_op jit(solution)/shard_map/all_to_all | solution.py:177
  207.4 19.5 %all-to-all-done.5 = f32[2,256,8,128]{3,0,2,1:T(2,128)S(1)} async-done(((f32[2,256,8,128]{3,0,2,1:T(2,128)}), f32[2,256,8,128]{3,0,2,1:T(2,128)S(1)}, u32[]{:S(2)}, u32[]{:S(2)}) %all-to-all-start.5) | async-done | bytes 2097184 | tf_op jit(solution)/shard_map/all_to_all | solution.py:177
  228.7 8.7 %all-reduce.6 = (f32[4096]{0:T(1024)S(1)}, f32[512]{0:T(512)S(1)}, f32[512]{0:T(512)S(1)}) all-reduce(f32[4096]{0:T(1024)S(1)} %bitcast.216, f32[512]{0:T(512)S(1)} %bitcast.218, f32[512]{0:T(512)S(1)} %bitcast.217), channel_id=3, replica_groups=mesh['rep'=4,'fsdp'=2,'ctx'=4] {'fsdp'}, use_global_device_ids=true, to_apply=%region_25.26.clone | all-reduce | flops 5120 | bytes 40960
  237.6 1.3 convert_element_type.261
  238.8 10.1 %all-reduce.4 = (f32[2048]{0:T(1024)S(1)}, f32[256]{0:T(256)S(1)}, f32[256]{0:T(256)S(1)}) all-reduce(f32[2048]{0:T(1024)S(1)} %dynamic-slice.250, f32[256]{0:T(256)S(1)} %dynamic-slice.252, f32[256]{0:T(256)S(1)} %dynamic-slice.254), channel_id=1, replica_groups=mesh['rep'=4,'fsdp'=2,'ctx'=4] {'ctx'}, use_global_device_ids=true, to_apply=%region_24.25 | all-reduce | flops 2560 | bytes 20480 | tf_op jit(solution)/shard_map/psum | solution.py:197
  248.9 19.5 %all-reduce.5 = (f32[2048]{0:T(1024)}, f32[256]{0:T(256)}, f32[256]{0:T(256)}) all-reduce(f32[2048]{0:T(1024)S(1)} %get-tuple-element.911, f32[256]{0:T(256)S(1)} %get-tuple-element.912, f32[256]{0:T(256)S(1)} %get-tuple-element.913), channel_id=1, replica_groups=mesh['rep'=4,'fsdp'=2,'ctx'=4] {'rep'}, use_global_device_ids=true, to_apply=%region_26.27 | all-reduce | flops 2560 | bytes 20480 | tf_op jit(solution)/shard_map/psum | solution.py:203
  (710 shorter events, 120.0 us)
Async XLA Ops:
  0.6 26.1 %copy-start = (bf16[2,64,512]{2,1,0:T(8,128)(2,1)S(1)}, bf16[2,64,512]{2,1,0:T(8,128)(2,1)}, u32[]{:S(2)}) copy-start(bf16[2,64,512]{2,1,0:T(8,128)(2,1)} %param.51) | copy-start | bytes 393220
  1.4 1.8 copy-start.9
  1.4 1.8 copy-start.5
  3.5 4.7 %copy-start.12 = (s32[2,64]{1,0:T(2,128)S(1)}, s32[2,64]{1,0:T(2,128)}, u32[]{:S(2)}) copy-start(s32[2,64]{1,0:T(2,128)} %param.57) | copy-start | bytes 1540
  3.5 5.4 %copy-start.14 = (u32[32]{0:T(128)S(1)}, u32[32]{0:T(128)}, u32[]{:S(2)}) copy-start(u32[32]{0:T(128)} %constant.749) | copy-start | bytes 388
  3.5 12.1 %copy-start.6 = (bf16[2,64,4096]{2,1,0:T(8,128)(2,1)S(1)}, bf16[2,64,4096]{2,1,0:T(8,128)(2,1)}, u32[]{:S(2)}) copy-start(bf16[2,64,4096]{2,1,0:T(8,128)(2,1)} %param.49) | copy-start | bytes 3145732
  5.0 17.3 %all-to-all-start.4 = ((f32[4,1,1024]{2,1,0:T(1,128)}), f32[4,1,1024]{2,1,0:T(1,128)S(1)}, u32[]{:S(2)}, u32[]{:S(2)}) async-start(f32[4,1,1024]{2,1,0:T(1,128)} %reshape.1247), calls=%async_computation.4 | async-start | bytes 32768 | tf_op jit(solution)/shard_map/all_to_all | solution.py:93
  14.9 0.8 copy-start.8
  19.3 1.8 copy-start.3
  21.1 14.1 %copy-start.1 = (bf16[2,64,32,64]{3,2,1,0:T(8,128)(2,1)S(1)}, bf16[2,64,32,64]{3,2,1,0:T(8,128)(2,1)}, u32[]{:S(2)}) copy-start(bf16[2,64,32,64]{3,2,1,0:T(8,128)(2,1)} %get-tuple-element.971) | copy-start | bytes 1572868
  22.3 7.4 %all-to-all-start.1 = ((bf16[2,64,4,128]{3,1,0,2:T(8,128)(2,1)}), bf16[2,64,4,128]{3,1,0,2:T(8,128)(2,1)S(1)}, u32[]{:S(2)}, u32[]{:S(2)}) async-start(bf16[2,64,4,128]{3,1,0,2:T(8,128)(2,1)} %copy.91), calls=%async_computation.1 | async-start | bytes 262144 | tf_op jit(solution)/shard_map/all_to_all | solution.py:89
  29.7 8.6 %all-to-all-start.3 = ((bf16[2,64,4,128]{3,1,0,2:T(8,128)(2,1)}), bf16[2,64,4,128]{3,1,0,2:T(8,128)(2,1)}, u32[]{:S(2)}, u32[]{:S(2)}) async-start(bf16[2,64,4,128]{3,1,0,2:T(8,128)(2,1)} %copy_bitcast_fusion.5), calls=%async_computation.3 | async-start | bytes 262144 | tf_op jit(solution)/shard_map/all_to_all | solution.py:90
  35.8 7.6 %copy-start.2 = (bf16[2,64,4096]{2,1,0:T(8,128)(2,1)S(1)}, bf16[2,64,4096]{2,1,0:T(8,128)(2,1)}, u32[]{:S(2)}) copy-start(bf16[2,64,4096]{2,1,0:T(8,128)(2,1)} %param.53) | copy-start | bytes 3145732
  35.8 7.6 %copy-start.10 = (f32[2,64]{1,0:T(2,128)S(1)}, f32[2,64]{1,0:T(2,128)}, u32[]{:S(2)}) copy-start(f32[2,64]{1,0:T(2,128)} %copy-done.9) | copy-start | bytes 1540
  38.3 17.9 %all-to-all-start = ((bf16[2,64,32,128]{3,1,0,2:T(8,128)(2,1)}), bf16[2,64,32,128]{3,1,0,2:T(8,128)(2,1)S(1)}, u32[]{:S(2)}, u32[]{:S(2)}) async-start(bf16[2,64,32,128]{3,1,0,2:T(8,128)(2,1)} %copy.89), calls=%async_computation | async-start | bytes 2097152 | tf_op jit(solution)/shard_map/all_to_all | solution.py:88
  43.4 17.9 %copy-start.11 = (s32[2,64]{1,0:T(2,128)S(1)}, s32[2,64]{1,0:T(2,128)}, u32[]{:S(2)}) copy-start(s32[2,64]{1,0:T(2,128)} %param.56) | copy-start | bytes 1540
  56.2 22.3 %all-to-all-start.2 = ((bf16[2,64,32,128]{3,1,0,2:T(8,128)(2,1)}), bf16[2,64,32,128]{3,1,0,2:T(8,128)(2,1)S(1)}, u32[]{:S(2)}, u32[]{:S(2)}) async-start(bf16[2,64,32,128]{3,1,0,2:T(8,128)(2,1)} %copy_bitcast_fusion.1), calls=%async_computation.2 | async-start | bytes 2097152 | tf_op jit(solution)/shard_map/all_to_all | solution.py:91
  181.3 7.9 %all-to-all-start.7 = ((bf16[2,256,1,128]{3,0,2,1:T(2,128)(2,1)}), bf16[2,256,1,128]{3,0,2,1:T(2,128)(2,1)S(1)}, u32[]{:S(2)}, u32[]{:S(2)}) async-start(bf16[2,256,1,128]{3,0,2,1:T(2,128)(2,1)} %bitcast.118), calls=%async_computation.7 | async-start | bytes 262144 | tf_op jit(solution)/shard_map/all_to_all | solution.py:179
  197.5 5.4 %copy-start.13 = (u32[32]{0:T(128)S(1)}, u32[32]{0:T(128)}, u32[]{:S(2)}) copy-start(u32[32]{0:T(128)} %constant.755) | copy-start | bytes 388
  197.5 8.6 %copy-start.4 = (f32[2,64,64]{2,1,0:T(8,128)S(1)}, f32[2,64,64]{2,1,0:T(8,128)}, u32[]{:S(2)}) copy-start(f32[2,64,64]{2,1,0:T(8,128)} %copy-done.3) | copy-start | bytes 98308
  197.5 8.6 %copy-start.7 = (f32[2,64,64]{2,1,0:T(8,128)S(1)}, f32[2,64,64]{2,1,0:T(8,128)}, u32[]{:S(2)}) copy-start(f32[2,64,64]{2,1,0:T(8,128)} %get-tuple-element.976) | copy-start | bytes 98308
  197.5 29.4 %all-to-all-start.5 = ((f32[2,256,8,128]{3,0,2,1:T(2,128)}), f32[2,256,8,128]{3,0,2,1:T(2,128)S(1)}, u32[]{:S(2)}, u32[]{:S(2)}) async-start(f32[2,256,8,128]{3,0,2,1:T(2,128)} %get-tuple-element.751), calls=%async_computation.5 | async-start | bytes 4194304 | tf_op jit(solution)/shard_map/all_to_all | solution.py:177
where the time goes:
time: 272 us; the launch traced here: 268 us
  matrix products  66.3 us (24%)
  blocking collectives  64.7 us (24%)
  waiting for transfers between devices  37.1 us (14%)
  starting transfers between devices  33.8 us (12%)
  local copies, waits for them, and re-layouts  32 us (12%)
  other arithmetic  29.5 us (11%)
  between operations  2.89 us (1%)
    psum x1, blocking collectives, per_device(): bias_q, bias_k, bias_v = lax.psum((shares[0], shares[1], shares[2]), 'rep')  19.5 us
    all_to_all x1, waiting for transfers between devices, per_device(): lax.all_to_all(grad_q_all, 'ctx', split_axis=1, concat_axis=2, tiled=True)  19.5 us
    dot_general x64, matrix products, one_head(): jnp.einsum('lox,log->lxg', attention_reduced_precision, gradient_block_ro...  18.6 us
    dot_general x64, matrix products, one_head(): jnp.einsum('vlf,vwf->vlw', query_block_rows, key_block_rows, preferred_el...  14.5 us
    dot_general x64, matrix products, one_head(): jnp.einsum('lox,log->lxg', scores_gradient, query_block_rows, preferred_e...  13.9 us
    all_gather x1, blocking collectives, per_device(): seg_all = lax.all_gather(segment_ids, 'ctx', axis=1, tiled=True)  13.7 us
    unnamed x2, blocking collectives  13 us
    all_to_all x1, waiting for transfers between devices, per_device(): lax.all_to_all(q_rot, 'ctx', split_axis=2, concat_axis=1, tiled=True)  11.5 us
  transfers between devices with their start and end apart: 7, of which 5 were waited for; matrix products, arithmetic and copies ran while one was open for 7% of the time, Pallas kernels for 0%

commit v1 on v0

v1 whole, which is shorter than its diff:
```python
import functools
import math

import jax
import jax.numpy as jnp
from jax import lax
from jax.experimental import pallas as pl
from jax.experimental.pallas import tpu as pltpu
from jax.sharding import PartitionSpec as P

HQ = 32
HK = 4
HD = 128
GROUP = HQ // HK
ROPE_BASE = 1000000.0
F32 = jnp.float32
BF16 = jnp.bfloat16
MESH = pl.DeviceIdType.MESH
NT = (((1,), (1,)), ((), ()))
TN = (((0,), (0,)), ((), ()))


def bias_layout(fsdps):
    q_rows, kv_rows = HQ // fsdps, max(1, HK // fsdps)
    return q_rows, kv_rows, -(-(q_rows + 2 * kv_rows) // 8) * 8


def rope(x, cos, sin):
    return x * cos + pltpu.roll(x, HD // 2, 1) * sin


def kernel(
    sizes,
    q_hbm, k_hbm, v_hbm, o_hbm, up_hbm, adv_ref, act_ref, seg_ref, code_ref,
    gq_hbm, gk_ref, gv_ref, bq_ref, bk_ref, bv_ref,
    q_in, o_in, up_in, k_all, v_all, code_all, seg_all,
    q_rot, g_low, delta, cos_tab, sin_tab, mask_tab,
    gq_out, part, own, exch, sums, arrive, bias_q, bias, bias_in, bias_half, bias_half_in,
    in_sem, out_sem, meta_send, meta_recv, kv_send, kv_recv, fw_send, fw_recv,
    ex_send, ex_recv, cr_send, cr_recv, b1_send, b1_recv, b2_send, b2_recv,
):
    n, reps, fsdps, seqs, toks = sizes
    length = n * toks
    pairs = n // 2
    chunks = seqs * HK
    width = GROUP * HD
    lanes = GROUP * toks
    scale = HD ** -0.5
    me = lax.axis_index("ctx")
    rep = lax.axis_index("rep")
    fs = lax.axis_index("fsdp")
    pair = me // 2
    core = me % 2
    buddy = me + 1 - 2 * core
    here = rep * fsdps + fs
    others = reps * fsdps
    q_rows, kv_rows, bias_rows = bias_layout(fsdps)

    def ctx_device(index):
        return {"ctx": index}

    def far_device(step):
        target = (here + step) % others
        return {"rep": target // fsdps, "fsdp": target % fsdps}

    def rows(index):
        return pl.ds(pl.multiple_of(index * toks, toks), toks)

    def cols(group):
        return pl.ds(pl.multiple_of(group * HD, HD), HD)

    def wide(group):
        return pl.ds(pl.multiple_of(group * width, width), width)

    loads = []
    for seq in range(seqs):
        loads.append(pltpu.make_async_copy(up_hbm.at[seq], up_in.at[seq], in_sem.at[0, seq]))
        loads.append(pltpu.make_async_copy(o_hbm.at[seq], o_in.at[seq], in_sem.at[1, seq]))
    for seq in range(seqs):
        loads.append(pltpu.make_async_copy(q_hbm.at[seq], q_in.at[seq], in_sem.at[2, seq]))
        loads.append(pltpu.make_async_copy(k_hbm.at[seq], k_all.at[seq, rows(me)], in_sem.at[3, seq]))
        loads.append(pltpu.make_async_copy(v_hbm.at[seq], v_all.at[seq, rows(me)], in_sem.at[4, seq]))
    for load in loads:
        load.start()

    barrier = pltpu.get_barrier_semaphore()
    for step in range(1, n):
        pl.semaphore_signal(barrier, inc=1, device_id=ctx_device((me + step) % n), device_id_type=MESH)
    for step in range(1, others):
        pl.semaphore_signal(barrier, inc=1, device_id=far_device(step), device_id_type=MESH)

    def clear(index, _):
        for seq in range(seqs):
            k_all[seq, rows(index), :] = jnp.zeros((toks, HK * HD), BF16)
            v_all[seq, rows(index), :] = jnp.zeros((toks, HK * HD), BF16)
        code_all[index] = jnp.zeros((seqs, toks), jnp.int32)
        seg_all[index] = jnp.zeros((seqs, toks), jnp.int32)
        return 0

    lax.fori_loop(me + 1, n, clear, 0)
    code_all[me] = code_ref[...]
    seg_all[me] = seg_ref[...]

    pl.semaphore_wait(barrier, n - 1 + others - 1)

    def meta_copy(source, target, slot):
        a = pltpu.make_async_remote_copy(
            code_ref, code_all.at[source], meta_send.at[0, slot], meta_recv.at[0, source],
            device_id=ctx_device(target), device_id_type=MESH)
        b = pltpu.make_async_remote_copy(
            seg_ref, seg_all.at[source], meta_send.at[1, slot], meta_recv.at[1, source],
            device_id=ctx_device(target), device_id_type=MESH)
        return a, b

    def meta_start(target, _):
        for copy in meta_copy(me, target, target):
            copy.start()
        return 0

    lax.fori_loop(me + 1, n, meta_start, 0)

    def kv_copy(source, target, slot, chunk, send, recv, forward):
        seq, group = chunk // HK, chunk % HK
        made = []
        for kind, (hbm, held) in enumerate(((k_hbm, k_all), (v_hbm, v_all))):
            place = held.at[seq, rows(source), cols(group)]
            origin = place if forward else hbm.at[seq, :, cols(group)]
            made.append(pltpu.make_async_remote_copy(
                origin, place, send.at[kind, slot, chunk], recv.at[kind, source, chunk],
                device_id=ctx_device(target), device_id_type=MESH))
        return made

    def kv_start(chunk, _):
        def later(other, _):
            for copy in kv_copy(me, 2 * other + core, other, chunk, kv_send, kv_recv, False):
                copy.start()
            return 0

        lax.fori_loop(pair + 1, pairs, later, 0)

        @pl.when(core == 0)
        def _():
            for copy in kv_copy(me, buddy, pair, chunk, kv_send, kv_recv, False):
                copy.start()
        return 0

    lax.fori_loop(0, chunks, kv_start, 0)

    eye = lax.broadcasted_iota(jnp.int32, (toks, toks), 0) == lax.broadcasted_iota(
        jnp.int32, (toks, toks), 1)

    def column(row):
        return jnp.sum(jnp.where(eye, row, 0.0), axis=1, keepdims=True)

    weight_rows = adv_ref[...] * act_ref[...].astype(F32)
    ones = jnp.ones((8, HD), BF16)
    for seq in range(seqs):
        weight = column(weight_rows[seq:seq + 1, :])
        loads[2 * seq].wait()
        loads[2 * seq + 1].wait()

        def cotangent(group, _, seq=seq, weight=weight):
            chunk = seq * HK + group
            up = up_in[seq, :, wide(group)]
            out = o_in[seq, :, wide(group)]
            high, low = [], []
            for head in range(GROUP):
                part_cols = slice(head * HD, (head + 1) * HD)
                rounded = (weight * up[:, part_cols].astype(F32)).astype(BF16)
                g_low[chunk, head * toks:(head + 1) * toks, :] = rounded
                product = rounded.astype(F32) * out[:, part_cols].astype(F32)
                top = product.astype(BF16)
                high.append(top)
                low.append((product - top.astype(F32)).astype(BF16))
            total = lax.dot_general(ones, jnp.concatenate(high, axis=0), NT, preferred_element_type=F32)
            total += lax.dot_general(ones, jnp.concatenate(low, axis=0), NT, preferred_element_type=F32)
            delta[chunk] = total
            return 0

        lax.fori_loop(0, HK, cotangent, 0)

    def meta_wait(source, _):
        for copy in meta_copy(source, me, 0):
            copy.wait_recv()
        return 0

    lax.fori_loop(0, me, meta_wait, 0)
    row_of = lax.broadcasted_iota(jnp.int32, (length, toks), 0)
    col_of = lax.broadcasted_iota(jnp.int32, (length, toks), 1)
    lane = lax.broadcasted_iota(jnp.int32, (1, HD), 1)
    first = lane < HD // 2
    key_index = lax.broadcasted_iota(jnp.int32, (length, lanes), 0)
    query_index = lax.broadcasted_iota(jnp.int32, (length, lanes), 1) % toks + me * toks
    causal = key_index <= query_index
    spread = (lax.broadcasted_iota(jnp.int32, (toks, lanes), 0)
              == lax.broadcasted_iota(jnp.int32, (toks, lanes), 1) % toks).astype(F32)
    position = []
    for seq in range(seqs):
        count = jnp.zeros((length, toks), F32)
        seg_columns = []
        for block in range(n):
            starts = jnp.where(code_all[block][seq:seq + 1, :] <= 1, 1.0, 0.0)
            count = count + jnp.where(col_of + block * toks <= row_of, starts, 0.0)
            seg_columns.append(column(seg_all[block][seq:seq + 1, :].astype(F32)))
        position.append(jnp.sum(count, axis=1, keepdims=True) - 1.0)
        seg_keys = jnp.concatenate(seg_columns, axis=0)
        seg_own = column(seg_ref[...][seq:seq + 1, :].astype(F32))
        seg_queries = jnp.sum(spread * seg_own, axis=0, keepdims=True)
        mask_tab[seq] = jnp.where(causal & (seg_keys == seg_queries), 0.0, -jnp.inf)
    half = (lane % (HD // 2)).astype(F32)
    freq = jnp.exp(half * (-2.0 * math.log(ROPE_BASE) / HD))
    angle = jnp.where(first, position[0], position[1]) * freq
    cos, sin = jnp.cos(angle), jnp.sin(angle)
    cos_swap, sin_swap = pltpu.roll(cos, HD // 2, 1), pltpu.roll(sin, HD // 2, 1)
    cos_tab[0] = jnp.where(first, cos, cos_swap)
    cos_tab[1] = jnp.where(first, cos_swap, cos)
    sin_tab[0] = jnp.where(first, -sin, sin_swap)
    sin_tab[1] = jnp.where(first, -sin_swap, sin)

    for index in range(2 * seqs, len(loads)):
        loads[index].wait()

    def query(chunk, _):
        seq, group = chunk // HK, chunk % HK
        raw = q_in[seq, :, wide(group)]
        c, s = cos_tab[seq, rows(me), :], sin_tab[seq, rows(me), :]
        for head in range(GROUP):
            piece = raw[:, head * HD:(head + 1) * HD].astype(F32)
            q_rot[chunk, head * toks:(head + 1) * toks, :] = rope(piece, c, s).astype(BF16)
        return 0

    lax.fori_loop(0, chunks, query, 0)

    def hand_on(chunk):
        def earlier(other, _):
            source = 2 * other + core
            for copy in kv_copy(source, me, 0, chunk, kv_send, kv_recv, False):
                copy.wait_recv()
            for copy in kv_copy(source, buddy, other, chunk, fw_send, fw_recv, True):
                copy.start()
            return 0

        lax.fori_loop(0, pair, earlier, 0)

    def take(chunk):
        def earlier(other, _):
            source = 2 * other + 1 - core
            for copy in kv_copy(source, me, 0, chunk, fw_send, fw_recv, False):
                copy.wait_recv()
            return 0

        lax.fori_loop(0, pair, earlier, 0)

        @pl.when(core == 1)
        def _():
            for copy in kv_copy(buddy, me, 0, chunk, kv_send, kv_recv, False):
                copy.wait_recv()

    def exchange(chunk, other, owner):
        return pltpu.make_async_remote_copy(
            part.at[chunk, owner], exch.at[chunk, other],
            ex_send.at[chunk, other], ex_recv.at[chunk, other],
            device_id=ctx_device(buddy), device_id_type=MESH)

    def cross(chunk, slot, other):
        return pltpu.make_async_remote_copy(
            sums.at[chunk, other], arrive.at[chunk, slot],
            cr_send.at[chunk, other], cr_recv.at[chunk, slot],
            device_id=ctx_device(2 * other + core), device_id_type=MESH)

    def pass_down(chunk):
        def earlier(other, _):
            exchange(chunk, other, 0).wait_recv()
            sums[chunk, other] = (part[chunk, 2 * other + core].astype(F32)
                                  + exch[chunk, other].astype(F32)).astype(BF16)
            cross(chunk, pair, other).start()
            return 0

        lax.fori_loop(0, pair, earlier, 0)

    bias_q[...] = jnp.zeros_like(bias_q)

    def attend(chunk, _):
        seq, group = chunk // HK, chunk % HK

        @pl.when(chunk + 1 < chunks)
        def _():
            hand_on(chunk + 1)

        take(chunk)
        keys = rope(k_all[seq, :, cols(group)].astype(F32), cos_tab[seq], sin_tab[seq]).astype(BF16)
        values = v_all[seq, :, cols(group)]
        queries, grads = q_rot[chunk], g_low[chunk]
        scores = lax.dot_general(keys, queries, NT, preferred_element_type=F32) + mask_tab[seq]
        top = jnp.max(scores, axis=0, keepdims=True)
        weights = jnp.exp((scores - top) * scale)
        probs = weights * (1.0 / jnp.sum(weights, axis=0, keepdims=True))
        grad_v = jnp.dot(probs.astype(BF16), grads, preferred_element_type=F32)
        grad_p = lax.dot_general(values, grads, NT, preferred_element_type=F32)
        grad_s = (probs * (grad_p - delta[chunk][0:1, :])).astype(BF16)
        grad_k = jnp.dot(grad_s, queries, preferred_element_type=F32) * scale
        grad_q = lax.dot_general(grad_s, keys, TN, preferred_element_type=F32) * scale
        for block in range(n):
            part[chunk, block, 0] = grad_k[block * toks:(block + 1) * toks].astype(BF16)
            part[chunk, block, 1] = grad_v[block * toks:(block + 1) * toks].astype(BF16)

            @pl.when(me == block)
            def _():
                own[chunk, 0] = grad_k[block * toks:(block + 1) * toks]
                own[chunk, 1] = grad_v[block * toks:(block + 1) * toks]

        def earlier(other, _):
            exchange(chunk, other, 2 * other + 1 - core).start()
            return 0

        lax.fori_loop(0, pair, earlier, 0)

        @pl.when(core == 1)
        def _():
            exchange(chunk, pair, buddy).start()

        c, s = cos_tab[seq, rows(me), :], sin_tab[seq, rows(me), :]
        totals, outs = [], []
        for head in range(GROUP):
            rounded = rope(grad_q[head * toks:(head + 1) * toks], c, -s).astype(BF16)
            outs.append(rounded)
            totals.append(jnp.sum(rounded.astype(F32), axis=0, keepdims=True))
        gq_out[chunk] = jnp.concatenate(outs, axis=1)
        bias_q[group] += jnp.concatenate(totals, axis=0)
        pltpu.make_async_copy(gq_out.at[chunk], gq_hbm.at[seq, :, wide(group)], out_sem.at[chunk]).start()

        @pl.when(chunk >= 1)
        def _():
            pass_down(chunk - 1)
        return 0

    hand_on(0)
    lax.fori_loop(0, chunks, attend, 0)
    pass_down(chunks - 1)

    bias_kv = [[jnp.zeros((1, HD), F32) for _ in range(HK)] for _ in range(2)]
    for chunk in range(chunks):
        seq, group = chunk // HK, chunk % HK

        @pl.when(core == 0)
        def _():
            exchange(chunk, pair, 0).wait_recv()
            own[chunk] += exch[chunk, pair].astype(F32)

        def incoming(other, _):
            cross(chunk, other, 0).wait_recv()
            own[chunk] += arrive[chunk, other].astype(F32)
            return 0

        lax.fori_loop(pair + 1, pairs, incoming, 0)
        c, s = cos_tab[seq, rows(me), :], sin_tab[seq, rows(me), :]
        key_grad = rope(own[chunk, 0], c, -s).astype(BF16)
        value_grad = own[chunk, 1].astype(BF16)
        gk_ref[seq, :, group * HD:(group + 1) * HD] = key_grad
        gv_ref[seq, :, group * HD:(group + 1) * HD] = value_grad
        bias_kv[0][group] += jnp.sum(key_grad.astype(F32), axis=0, keepdims=True)
        bias_kv[1][group] += jnp.sum(value_grad.astype(F32), axis=0, keepdims=True)
    heads_q = jnp.concatenate([bias_q[group] for group in range(HK)], axis=0)
    for shard in range(fsdps):
        lead = shard * HK // fsdps
        pieces = [heads_q[shard * q_rows:(shard + 1) * q_rows]]
        pieces += bias_kv[0][lead:lead + kv_rows] + bias_kv[1][lead:lead + kv_rows]
        pieces.append(jnp.zeros((bias_rows - q_rows - 2 * kv_rows, HD), F32))
        bias[shard] = jnp.concatenate(pieces, axis=0)

    def over_ctx(step, target):
        return pltpu.make_async_remote_copy(
            bias, bias_in.at[step], b1_send.at[step], b1_recv.at[step],
            device_id=ctx_device(target), device_id_type=MESH)

    for step in range(1, n):
        over_ctx(step, (me + step) % n).start()
    total = bias[...]
    for step in range(1, n):
        over_ctx(step, me).wait_recv()
        total = total + bias_in[step]
    bias_half[...] = total

    def over_rest(step):
        device = far_device(step)
        return pltpu.make_async_remote_copy(
            bias_half.at[device["fsdp"]], bias_half_in.at[step], b2_send.at[step], b2_recv.at[step],
            device_id=device, device_id_type=MESH)

    for step in range(1, others):
        over_rest(step).start()
    final = bias_half[fs]
    for step in range(1, others):
        over_rest(step).wait_recv()
        final = final + bias_half_in[step]
    bq_ref[...] = final[0:q_rows]
    bk_ref[...] = final[q_rows:q_rows + kv_rows]
    bv_ref[...] = final[q_rows + kv_rows:q_rows + 2 * kv_rows]

    def meta_end(target, _):
        for copy in meta_copy(me, target, target):
            copy.wait_send()
        return 0

    lax.fori_loop(me + 1, n, meta_end, 0)

    def end(chunk, _):
        def later(other, _):
            for copy in kv_copy(me, 2 * other + core, other, chunk, kv_send, kv_recv, False):
                copy.wait_send()
            return 0

        lax.fori_loop(pair + 1, pairs, later, 0)

        def earlier(other, _):
            for copy in kv_copy(2 * other + core, buddy, other, chunk, fw_send, fw_recv, True):
                copy.wait_send()
            exchange(chunk, other, 2 * other + 1 - core).wait_send()
            cross(chunk, pair, other).wait_send()
            return 0

        lax.fori_loop(0, pair, earlier, 0)

        @pl.when(core == 0)
        def _():
            for copy in kv_copy(me, buddy, pair, chunk, kv_send, kv_recv, False):
                copy.wait_send()

        @pl.when(core == 1)
        def _():
            exchange(chunk, pair, buddy).wait_send()

        pltpu.make_async_copy(
            gq_out.at[chunk], gq_hbm.at[chunk // HK, :, wide(chunk % HK)], out_sem.at[chunk]).wait()
        return 0

    lax.fori_loop(0, chunks, end, 0)
    for step in range(1, n):
        over_ctx(step, me).wait_send()
    for step in range(1, others):
        over_rest(step).wait_send()


def per_device(sizes, *args):
    n, reps, fsdps, seqs, toks = sizes
    length, pairs, chunks = n * toks, n // 2, seqs * HK
    rows, width, others = GROUP * toks, HQ * HD, reps * fsdps
    q_rows, kv_rows, bias_rows = bias_layout(fsdps)
    dma = pltpu.SemaphoreType.DMA
    vmem = pl.BlockSpec(memory_space=pltpu.VMEM)
    anywhere = pl.BlockSpec(memory_space=pl.ANY)
    out = pl.pallas_call(
        functools.partial(kernel, sizes),
        out_shape=(
            jax.ShapeDtypeStruct((seqs, toks, HQ * HD), BF16),
            jax.ShapeDtypeStruct((seqs, toks, HK * HD), BF16),
            jax.ShapeDtypeStruct((seqs, toks, HK * HD), BF16),
            jax.ShapeDtypeStruct((q_rows, HD), F32),
            jax.ShapeDtypeStruct((kv_rows, HD), F32),
            jax.ShapeDtypeStruct((kv_rows, HD), F32),
        ),
        in_specs=[anywhere] * 5 + [vmem] * 4,
        out_specs=(anywhere, vmem, vmem, vmem, vmem, vmem),
        scratch_shapes=[
            pltpu.VMEM((seqs, toks, width), BF16),
            pltpu.VMEM((seqs, toks, width), BF16),
            pltpu.VMEM((seqs, toks, width), BF16),
            pltpu.VMEM((seqs, length, HK * HD), BF16),
            pltpu.VMEM((seqs, length, HK * HD), BF16),
            pltpu.VMEM((n, seqs, toks), jnp.int32),
            pltpu.VMEM((n, seqs, toks), jnp.int32),
            pltpu.VMEM((chunks, rows, HD), BF16),
            pltpu.VMEM((chunks, rows, HD), BF16),
            pltpu.VMEM((chunks, 8, rows), F32),
            pltpu.VMEM((seqs, length, HD), F32),
            pltpu.VMEM((seqs, length, HD), F32),
            pltpu.VMEM((seqs, length, rows), F32),
            pltpu.VMEM((chunks, toks, GROUP * HD), BF16),
            pltpu.VMEM((chunks, n, 2, toks, HD), BF16),
            pltpu.VMEM((chunks, 2, toks, HD), F32),
            pltpu.VMEM((chunks, pairs, 2, toks, HD), BF16),
            pltpu.VMEM((chunks, pairs, 2, toks, HD), BF16),
            pltpu.VMEM((chunks, pairs, 2, toks, HD), BF16),
            pltpu.VMEM((HK, GROUP, HD), F32),
            pltpu.VMEM((fsdps, bias_rows, HD), F32),
            pltpu.VMEM((n, fsdps, bias_rows, HD), F32),
            pltpu.VMEM((fsdps, bias_rows, HD), F32),
            pltpu.VMEM((others, bias_rows, HD), F32),
            dma((5, seqs)),
            dma((chunks,)),
            dma((2, n)),
            dma((2, n)),
            dma((2, pairs, chunks)),
            dma((2, n, chunks)),
            dma((2, pairs, chunks)),
            dma((2, n, chunks)),
            dma((chunks, pairs)),
            dma((chunks, pairs)),
            dma((chunks, pairs)),
            dma((chunks, pairs)),
            dma((n,)),
            dma((n,)),
            dma((others,)),
            dma((others,)),
        ],
        compiler_params=pltpu.CompilerParams(
            collective_id=0, has_side_effects=True, vmem_limit_bytes=60 * 1024 * 1024
        ),
        name="attention_backward",
    )(*args)
    flat = [part.reshape(-1) for part in out[3:]]
    share = HK * HD // fsdps
    if share < HD:
        begin = (lax.axis_index("fsdp") * share) % HD
        flat[1:] = [lax.dynamic_slice(part, (begin,), (share,)) for part in flat[1:]]
    return out[:3] + tuple(flat)


def solution(mesh):
    tokens = P(("rep", "fsdp"), "ctx", None)
    flat = P(("rep", "fsdp"), "ctx")
    shape = dict(mesh.shape)

    def run(*args):
        n, reps, fsdps = shape["ctx"], shape["rep"], shape["fsdp"]
        sizes = (n, reps, fsdps, args[0].shape[0] // (reps * fsdps), args[0].shape[1] // n)
        return jax.shard_map(
            functools.partial(per_device, sizes),
            mesh=mesh,
            in_specs=(tokens,) * 5 + (flat,) * 4,
            out_specs=(tokens, tokens, tokens, P("fsdp"), P("fsdp"), P("fsdp")),
            check_vma=False,
        )(*args)

    return run
```

time: 272 us -> 40.5 us (0.15); the launches traced: 268 us -> 40.3 us
  matrix products: 66.3 us -> 0 us
  blocking collectives: 64.7 us -> 0 us
  waiting for transfers between devices: 37.1 us -> 0 us
  Pallas kernels: 0 us -> 33.8 us
  starting transfers between devices: 33.8 us -> 0 us
  other arithmetic: 29.5 us -> 0 us
  local copies, waits for them, and re-layouts: 32 us -> 5.86 us
    dot_general x320 -> x0, matrix products: 66.3 us -> none  [the longest x64 18.6 us: one_head(): jnp.einsum('lox,log->lxg', attention_reduced_precision, gradient_block_ro...]
    all_to_all x7 -> x0, waiting for transfers between devices: 37.1 us -> none  [the longest x1 19.5 us: per_device(): lax.all_to_all(grad_q_all, 'ctx', split_axis=1, concat_axis=2, tiled=True)]
    all_to_all x7 -> x0, starting transfers between devices: 33.8 us -> none  [the longest x1 5.53 us: per_device(): lax.all_to_all(v_wide, 'ctx', split_axis=2, concat_axis=1, tiled=True)]
    pallas_call x0 -> x1, Pallas kernels: none -> 33.8 us  [per_device(): pl.pallas_call(functools.partial(kernel, sizes), out_shape=(jax.ShapeDtyp...]
    psum x2 -> x0, blocking collectives: 29.6 us -> none  [the longest x1 19.5 us: per_device(): bias_q, bias_k, bias_v = lax.psum((shares[0], shares[1], shares[2]), 'rep')]
    all_gather x1 -> x0, blocking collectives: 13.7 us -> none  [per_device(): seg_all = lax.all_gather(segment_ids, 'ctx', axis=1, tiled=True)]
    unnamed x2 -> x0, blocking collectives: 13 us -> none
    reduce_sum x70 -> x0, other arithmetic: 12 us -> none  [the longest x64 9.97 us: one_head(): row_total = jnp.sum(jnp.exp(scores - row_max), axis=2, keepdims=True)]
  transfers between devices with their start and end apart: 7 -> 0, of which waited for: 5 -> 0; matrix products, arithmetic and copies ran while one was open for 7% -> 0% of each run, Pallas kernels for 0% -> 0%
where the time goes in v1:
time: 40.5 us; the launch traced here: 40.3 us
  Pallas kernels  33.8 us (83%)
  local copies, waits for them, and re-layouts  5.86 us (14%)
  between operations  0.66 us (2%)
    pallas_call x1, Pallas kernels, per_device(): pl.pallas_call(functools.partial(kernel, sizes), out_shape=(jax.ShapeDtyp...  33.8 us
    unnamed x16, local copies, waits for them, and re-layouts  5.86 us

profile of v1, /device:TPU:4, one launch (start us, length us, event | category | flops | bytes accessed | tf_op | source)
XLA Modules:
  0.0 40.3 jit_solution(10093784642532849764)
XLA Ops:
  0.6 33.8 %attention_backward.1 = (bf16[2,64,4096]{2,1,0:T(8,128)(2,1)}, bf16[2,64,512]{2,1,0:T(8,128)(2,1)}, bf16[2,64,512]{2,1,0:T(8,128)(2,1)}, f32[16,128]{1,0:T(8,128)}, f32[2,128]{1,0:T(2,128)}, /*index=5*/f32[2,128]{1,0:T(2,128)}) custom-call(bf16[2,64,4096]{2,1,0:T(8,128)(2,1)} %q_hbm.1, bf16[2,64,512]{2,1,0:T(8,128)(2,1)} %k_hbm.1, ...), custom_call_target="tpu_custom_call" | custom-call | tf_op jit(solution)/shard_map/attention_backward/pallas_call | solution.py:452
  34.4 0.0 copy-start.1
  34.4 2.3 %copy.21 = bf16[2,64,4096]{2,1,0:T(8,128)(2,1)} copy(bf16[2,64,4096]{2,1,0:T(8,128)(2,1)} %get-tuple-element.24) | data formatting | bytes 2097152
  36.7 0.0 copy-done.1
  36.7 0.0 copy-start
  36.8 0.7 %copy.22 = bf16[2,64,512]{2,1,0:T(8,128)(2,1)} copy(bf16[2,64,512]{2,1,0:T(8,128)(2,1)S(1)} %copy-done.1) | data formatting | bytes 262144
  37.4 0.3 copy-done
  37.7 0.0 copy-start.2
  37.7 0.7 %copy.23 = bf16[2,64,512]{2,1,0:T(8,128)(2,1)} copy(bf16[2,64,512]{2,1,0:T(8,128)(2,1)S(1)} %copy-done) | data formatting | bytes 262144
  38.4 0.0 copy-done.2
  38.4 0.0 copy-start.4
  38.4 0.6 %copy.24 = f32[2048]{0:T(1024)} copy(f32[2048]{0:T(1024)S(1)} %bitcast.3) | data formatting | bytes 16384
  39.0 0.1 copy-done.4
  39.1 0.0 copy-start.3
  39.1 0.6 %copy.25 = f32[256]{0:T(256)} copy(f32[256]{0:T(256)S(1)} %bitcast.5) | data formatting | bytes 2048
  39.6 0.1 copy-done.3
  39.7 0.6 %copy.26 = f32[256]{0:T(256)} copy(f32[256]{0:T(256)S(1)} %bitcast.4) | data formatting | bytes 2048
Async XLA Ops:
  34.4 2.3 %copy-start.1 = (bf16[2,64,512]{2,1,0:T(8,128)(2,1)S(1)}, bf16[2,64,512]{2,1,0:T(8,128)(2,1)}, u32[]{:S(2)}) copy-start(bf16[2,64,512]{2,1,0:T(8,128)(2,1)} %get-tuple-element.25) | copy-start | bytes 393220
  36.7 1.0 %copy-start = (bf16[2,64,512]{2,1,0:T(8,128)(2,1)S(1)}, bf16[2,64,512]{2,1,0:T(8,128)(2,1)}, u32[]{:S(2)}) copy-start(bf16[2,64,512]{2,1,0:T(8,128)(2,1)} %get-tuple-element.26) | copy-start | bytes 393220
  37.7 0.7 %copy-start.2 = (f32[16,128]{1,0:T(8,128)S(1)}, f32[16,128]{1,0:T(8,128)}, u32[]{:S(2)}) copy-start(f32[16,128]{1,0:T(8,128)} %get-tuple-element.15) | copy-start | bytes 24580
  38.4 0.7 %copy-start.4 = (f32[2,128]{1,0:T(2,128)S(1)}, f32[2,128]{1,0:T(2,128)}, u32[]{:S(2)}) copy-start(f32[2,128]{1,0:T(2,128)} %get-tuple-element.16) | copy-start | bytes 3076
  39.1 0.7 %copy-start.3 = (f32[2,128]{1,0:T(2,128)S(1)}, f32[2,128]{1,0:T(2,128)}, u32[]{:S(2)}) copy-start(f32[2,128]{1,0:T(2,128)} %get-tuple-element.17) | copy-start | bytes 3076

commit v2 on v1

--- a/solution.py
+++ b/solution.py
@@ -439,6 +439,31 @@
         over_ctx(step, me).wait_send()
     for step in range(1, others):
         over_rest(step).wait_send()
+
+
+PIECES = 4
+
+
+def finish(*refs):
+    made, wide_hbm = refs[:6], refs[6]
+    held, load_sem, store_sem = refs[12:]
+    results = refs[6:12]
+    seqs = made[0].shape[0]
+    span = made[0].shape[2] // PIECES
+    loads, stores = [], []
+    for piece in range(seqs * PIECES):
+        place = (piece // PIECES, slice(None), pl.ds(piece % PIECES * span, span))
+        loads.append(pltpu.make_async_copy(made[0].at[place], held.at[piece], load_sem.at[piece]))
+        stores.append(pltpu.make_async_copy(held.at[piece], wide_hbm.at[place], store_sem.at[piece]))
+    for load in loads:
+        load.start()
+    for source, result in zip(made[1:], results[1:]):
+        result[...] = source[...]
+    for load, store in zip(loads, stores):
+        load.wait()
+        store.start()
+    for store in stores:
+        store.wait()
 
 
 def per_device(sizes, *args):
@@ -508,6 +533,18 @@
         ),
         name="attention_backward",
     )(*args)
+    out = pl.pallas_call(
+        finish,
+        out_shape=tuple(jax.ShapeDtypeStruct(part.shape, part.dtype) for part in out),
+        in_specs=[anywhere] + [vmem] * 5,
+        out_specs=(anywhere,) + (vmem,) * 5,
+        scratch_shapes=[
+            pltpu.VMEM((seqs * PIECES, toks, width // PIECES), BF16),
+            dma((seqs * PIECES,)),
+            dma((seqs * PIECES,)),
+        ],
+        name="finish",
+    )(*out)
     flat = [part.reshape(-1) for part in out[3:]]
     share = HK * HD // fsdps
     if share < HD:

time: 40.5 us -> 38.4 us (0.948)
  local copies, waits for them, and re-layouts: 5.86 us -> 0 us
  Pallas kernels: 33.8 us -> 37.5 us
    unnamed x16 -> x0, local copies, waits for them, and re-layouts: 5.86 us -> none
    pallas_call x0 -> x1, Pallas kernels: none -> 3.77 us  [per_device(): pl.pallas_call(finish, out_shape=tuple((jax.ShapeDtypeStruct(part.shape,...]
where the time goes in v2:
time: 38.4 us; the launch traced here: 38.2 us
  Pallas kernels  37.5 us (98%)
  between operations  0.64 us (2%)
    pallas_call x1, Pallas kernels, per_device(): pl.pallas_call(functools.partial(kernel, sizes), out_shape=(jax.ShapeDtyp...  33.8 us
    pallas_call x1, Pallas kernels, per_device(): pl.pallas_call(finish, out_shape=tuple((jax.ShapeDtypeStruct(part.shape,...  3.77 us

profile of v2, /device:TPU:4, one launch (start us, length us, event | category | flops | bytes accessed | tf_op | source)
XLA Modules:
  0.0 38.2 jit_solution(3165528439398417149)
XLA Ops:
  0.6 33.8 %attention_backward.1 = (bf16[2,64,4096]{2,1,0:T(8,128)(2,1)}, bf16[2,64,512]{2,1,0:T(8,128)(2,1)}, bf16[2,64,512]{2,1,0:T(8,128)(2,1)}, f32[16,128]{1,0:T(8,128)}, f32[2,128]{1,0:T(2,128)}, /*index=5*/f32[2,128]{1,0:T(2,128)}) custom-call(bf16[2,64,4096]{2,1,0:T(8,128)(2,1)} %q_hbm.1, bf16[2,64,512]{2,1,0:T(8,128)(2,1)} %k_hbm.1, ...), custom_call_target="tpu_custom_call" | custom-call | tf_op jit(solution)/shard_map/attention_backward/pallas_call | solution.py:477
  34.4 3.8 %finish.1 = (bf16[2,64,4096]{2,1,0:T(8,128)(2,1)}, bf16[2,64,512]{2,1,0:T(8,128)(2,1)}, bf16[2,64,512]{2,1,0:T(8,128)(2,1)}, f32[16,128]{1,0:T(8,128)}, f32[2,128]{1,0:T(2,128)}, /*index=5*/f32[2,128]{1,0:T(2,128)}) custom-call(bf16[2,64,4096]{2,1,0:T(8,128)(2,1)} %get-tuple-element.18.refs_0_, bf16[2,64,512]{2,1,0:T(8,128)(2,1)} %get-tuple-element.19.refs_1_, ...), custom_call_target="tpu_custom_call" | custom-call | tf_op jit(solution)/shard_map/finish/pallas_call | solution.py:536

commit v3 on v2

--- a/solution.py
+++ b/solution.py
@@ -335,7 +335,7 @@
         return 0
 
     hand_on(0)
-    lax.fori_loop(0, chunks, attend, 0)
+    lax.fori_loop(0, chunks, attend, 0, unroll=2)
     pass_down(chunks - 1)
 
     bias_kv = [[jnp.zeros((1, HD), F32) for _ in range(HK)] for _ in range(2)]

time: 38.4 us -> 38.3 us (level)
  no operation moved by 1% of the time
where the time goes in v3:
time: 38.3 us; the launch traced here: 38.2 us
  Pallas kernels  37.5 us (98%)
  between operations  0.64 us (2%)
    pallas_call x1, Pallas kernels, per_device(): pl.pallas_call(functools.partial(kernel, sizes), out_shape=(jax.ShapeDtyp...  33.8 us
    pallas_call x1, Pallas kernels, per_device(): pl.pallas_call(finish, out_shape=tuple((jax.ShapeDtypeStruct(part.shape,...  3.77 us

profile of v3, /device:TPU:4, one launch (start us, length us, event | category | flops | bytes accessed | tf_op | source)
XLA Modules:
  0.0 38.2 jit_solution(13444759970414589203)
XLA Ops:
  0.6 33.8 %attention_backward.1 = (bf16[2,64,4096]{2,1,0:T(8,128)(2,1)}, bf16[2,64,512]{2,1,0:T(8,128)(2,1)}, bf16[2,64,512]{2,1,0:T(8,128)(2,1)}, f32[16,128]{1,0:T(8,128)}, f32[2,128]{1,0:T(2,128)}, /*index=5*/f32[2,128]{1,0:T(2,128)}) custom-call(bf16[2,64,4096]{2,1,0:T(8,128)(2,1)} %q_hbm.1, bf16[2,64,512]{2,1,0:T(8,128)(2,1)} %k_hbm.1, ...), custom_call_target="tpu_custom_call" | custom-call | tf_op jit(solution)/shard_map/attention_backward/pallas_call | solution.py:477
  34.4 3.8 %finish.1 = (bf16[2,64,4096]{2,1,0:T(8,128)(2,1)}, bf16[2,64,512]{2,1,0:T(8,128)(2,1)}, bf16[2,64,512]{2,1,0:T(8,128)(2,1)}, f32[16,128]{1,0:T(8,128)}, f32[2,128]{1,0:T(2,128)}, /*index=5*/f32[2,128]{1,0:T(2,128)}) custom-call(bf16[2,64,4096]{2,1,0:T(8,128)(2,1)} %get-tuple-element.18.refs_0_, bf16[2,64,512]{2,1,0:T(8,128)(2,1)} %get-tuple-element.19.refs_1_, ...), custom_call_target="tpu_custom_call" | custom-call | tf_op jit(solution)/shard_map/finish/pallas_call | solution.py:536
